TPU v7x, 32 devices: a whole 2x2x4 slice. The times are simulated.
32 devices in a mesh: dp: 4 (over x, core), ctx: 2 (over y), tensor: 4 (over z).
Axes of the slice: x: 2, y: 2, z: 4, core: 2. Of those that a mesh axis runs over, the one named last changes fastest.
Arguments:
- hidden_in: bfloat16 [8, 1024, 2048], P('dp', 'ctx'), may hold values from -36.5 to 36.5
- lengths: int32 [8], replicated, may hold values from 256 to 1024, as said below
- w_query: bfloat16 [2048, 2048], P(('dp', 'ctx'), 'tensor'), may hold values from -0.125 to 0.125
- w_keyval: bfloat16 [2048, 4, 128], P(('dp', 'ctx'), 'tensor'), may hold values from -0.125 to 0.125
- w_output: bfloat16 [2048, 2048], P(('dp', 'ctx'), 'tensor'), may hold values from -1.5 to 1.5
- w_gateup: bfloat16 [2048, 2, 5632], P(('dp', 'ctx'), None, 'tensor'), may hold values from -0.125 to 0.125
- w_down: bfloat16 [2048, 5632], P(('dp', 'ctx'), 'tensor'), may hold values from -0.078125 to 0.078125
- gain_attn: bfloat16 [2048], P(('dp', 'ctx')), may hold values from 0.5 to 1.5
- gain_mlp: bfloat16 [2048], P(('dp', 'ctx')), may hold values from 0.5 to 1.5
- cotangent: bfloat16 [8, 1024, 2048], P('dp', 'ctx'), may hold values from -6 to 6
Outputs:
- output: bfloat16 [8, 1024, 2048], P('dp', 'ctx')
- input_grad: bfloat16 [8, 1024, 2048], P('dp', 'ctx')
- grad_query: float32 [2048, 2048], P(('dp', 'ctx'), 'tensor')
- grad_keyval: float32 [2048, 4, 128], P(('dp', 'ctx'), 'tensor')
- grad_output: float32 [2048, 2048], P(('dp', 'ctx'), 'tensor')
- grad_gateup: float32 [2048, 2, 5632], P(('dp', 'ctx'), None, 'tensor')
- grad_down: float32 [2048, 5632], P(('dp', 'ctx'), 'tensor')
- grad_gain_attn: float32 [2048], P(('dp', 'ctx'))
- grad_gain_mlp: float32 [2048], P(('dp', 'ctx'))
- root_means: float32 [3], replicated
Inputs may be any that keep to these rules, and one draw needn't show every extreme that they name: `lengths`: in every draw the first slot has exactly 1024 valid tokens and the last exactly 256.
All inputs are finite; a program needn't handle non-finite values.
Results may differ from a plain program's by a relative error of at most 0.014.
Values may be sent and summed in bfloat16 or wider, within the bound.
No kernel may reach another device: no remote copies, remote signals or barrier semaphores. Data moves between devices by JAX's collectives and lax.ppermute only.
A program may use at most 384 MiB of HBM per device.

v0:
```python
import jax
import jax.numpy as jnp
from jax import lax
from jax.sharding import PartitionSpec as P

D = 2048
HD = 64
EPS = 1e-05
THETA = 10000.0
NEG_FILL = -1e30


def from_behind(block, axis, distance):
    devices = range(lax.axis_size(axis))
    route = [(i - distance, i) for i in devices if i - distance in devices]
    return lax.ppermute(block, axis, route)


def rms_scale(values):
    return lax.rsqrt(jnp.mean(values * values, axis=-1, keepdims=True) + EPS)


def rope_tables(positions, head_width):
    frequency = THETA ** (-jnp.arange(0, head_width, 2).astype(jnp.float32) / head_width)
    angles = positions.astype(jnp.float32)[:, None] * frequency[None, :]
    angles = jnp.concatenate([angles, angles], axis=-1)
    return (jnp.cos(angles), jnp.sin(angles))


def rotate(values, cosine, sine):
    half_width = values.shape[-1] // 2
    turned = jnp.concatenate([-values[..., half_width:], values[..., :half_width]], axis=-1)
    return values * cosine + turned * sine


def rotate_back(grads, cosine, sine):
    half_width = grads.shape[-1] // 2
    scaled = grads * sine
    turned = jnp.concatenate([scaled[..., half_width:], -scaled[..., :half_width]], axis=-1)
    return grads * cosine + turned


def contract_rows(left, right):
    return lax.dot_general(
        left, right, (((0,), (0,)), ((), ())), preferred_element_type=jnp.float32
    )


def contract_cols(left, right):
    return lax.dot_general(
        left, right, (((1,), (1,)), ((), ())), preferred_element_type=jnp.float32
    )


def score_block(queries, pair, positions, key_positions, length):
    allowed = (
        (key_positions[None, :] <= positions[:, None])
        & (key_positions[None, :] >= 0)
        & (key_positions[None, :] < length)
    )
    raw_scores = jnp.einsum(
        "qhd,pd->hqp", queries, pair[:, :HD], preferred_element_type=jnp.float32
    )
    return jnp.where(allowed[None], raw_scores * HD ** (-0.5), NEG_FILL)


def forward_step(weights, positions, key_positions, cosine, sine, squares, packed):
    query_w, keyval_w, output_w, gateup_w, down_w, attn_gain, mlp_gain = weights
    token_rows, length = packed
    tokens = token_rows.astype(jnp.float32)
    rows, width = tokens.shape
    heads = query_w.shape[1] // HD
    live_mask = (positions < length).astype(jnp.float32)[:, None]
    normed = (tokens * rms_scale(tokens) * attn_gain.astype(jnp.float32)).astype(jnp.bfloat16)
    query_lin = jnp.dot(normed, query_w, preferred_element_type=jnp.float32)
    keyval_lin = jnp.dot(normed, keyval_w.reshape(width, -1), preferred_element_type=jnp.float32)
    queries = rotate(
        query_lin.reshape(rows, heads, HD), cosine[:, None, :], sine[:, None, :]
    ).astype(jnp.bfloat16)
    keys = rotate(keyval_lin[:, :HD], cosine, sine)
    local_pair = jnp.concatenate([keys, keyval_lin[:, HD:]], axis=-1).astype(jnp.bfloat16)
    remote_pair = from_behind(local_pair, "ctx", 1)
    pair = jnp.concatenate([remote_pair, local_pair], axis=0)
    scores = score_block(queries, pair, positions, key_positions, length)
    top = jnp.max(scores, axis=-1, keepdims=True)
    shifted = jnp.exp(scores - top)
    total = jnp.sum(shifted, axis=-1, keepdims=True)
    attend = (shifted / total).astype(jnp.bfloat16)
    log_total = top + jnp.log(total)
    context = jnp.einsum("hqp,pd->qhd", attend, pair[:, HD:], preferred_element_type=jnp.float32)
    context = context.reshape(rows, heads * HD).astype(jnp.bfloat16)
    attn_part = contract_cols(context, output_w)
    attn_out = lax.psum(attn_part, "tensor")
    middle = tokens + attn_out
    normed_mlp = (middle * rms_scale(middle) * mlp_gain.astype(jnp.float32)).astype(jnp.bfloat16)
    gateup = jnp.dot(
        normed_mlp, gateup_w.reshape(width, -1), preferred_element_type=jnp.float32
    ).reshape(rows, 2, -1)
    hidden = (jax.nn.silu(gateup[:, 0]) * gateup[:, 1]).astype(jnp.bfloat16)
    mlp_part = contract_cols(hidden, down_w)
    mlp_out = lax.psum(mlp_part.astype(jnp.bfloat16), "tensor").astype(jnp.float32)
    result = (middle + mlp_out) * live_mask
    squares = squares + jnp.stack(
        [
            jnp.sum(result * result),
            jnp.sum(attn_out * attn_out * live_mask),
            jnp.sum(mlp_out * mlp_out * live_mask),
        ]
    )
    saved = (normed, queries, pair, log_total, context, middle, normed_mlp, gateup)
    return (squares, (result.astype(jnp.bfloat16), saved))


def backward_step(weights, positions, key_positions, cosine, sine, totals, packed):
    query_w, keyval_w, output_w, gateup_w, down_w, attn_gain, mlp_gain = weights
    token_rows, seed_rows, length, saved = packed
    normed, queries, pair, log_total, context, middle, normed_mlp, gateup = saved
    tokens = token_rows.astype(jnp.float32)
    rows, width = tokens.shape
    heads = queries.shape[1]
    live_mask = (positions < length).astype(jnp.float32)[:, None]
    seed = seed_rows.astype(jnp.float32) * live_mask
    mlp_seed = seed.astype(jnp.bfloat16)
    gate_lin = gateup[:, 0]
    up_lin = gateup[:, 1]
    sigmoid_gate = jax.nn.sigmoid(gate_lin)
    activated = jax.nn.silu(gate_lin)
    hidden = (activated * up_lin).astype(jnp.bfloat16)
    grad_hidden = jnp.dot(mlp_seed, down_w, preferred_element_type=jnp.float32)
    grad_gate = grad_hidden * up_lin * (sigmoid_gate * (1.0 + gate_lin * (1.0 - sigmoid_gate)))
    grad_up = grad_hidden * activated
    grad_gateup = jnp.stack([grad_gate, grad_up], axis=1).reshape(rows, -1).astype(jnp.bfloat16)
    gateup_flat = gateup_w.reshape(width, -1)
    mlp_back_part = contract_cols(grad_gateup, gateup_flat)
    grad_normed_mlp = lax.psum(mlp_back_part, "tensor")
    mlp_scale = rms_scale(middle)
    weighted_mlp = grad_normed_mlp * mlp_gain.astype(jnp.float32)
    grad_middle = (
        seed
        + mlp_scale * weighted_mlp
        - middle * mlp_scale**3 * jnp.mean(weighted_mlp * middle, axis=-1, keepdims=True)
    )
    seed_part_low = grad_middle.astype(jnp.bfloat16)
    grad_context = (
        jnp.dot(seed_part_low, output_w, preferred_element_type=jnp.float32)
        .astype(jnp.bfloat16)
        .reshape(rows, heads, HD)
    )
    scores = score_block(queries, pair, positions, key_positions, length)
    attend_full = jnp.exp(scores - log_total)
    grad_attend = jnp.einsum(
        "qhd,pd->hqp", grad_context, pair[:, HD:], preferred_element_type=jnp.float32
    )
    center = jnp.sum(attend_full * grad_attend, axis=-1, keepdims=True)
    grad_raw = (attend_full * (grad_attend - center) * HD ** (-0.5)).astype(jnp.bfloat16)
    grad_values = jnp.einsum(
        "hqp,qhd->pd",
        attend_full.astype(jnp.bfloat16),
        grad_context,
        preferred_element_type=jnp.float32,
    )
    grad_queries = jnp.einsum(
        "hqp,pd->qhd", grad_raw, pair[:, :HD], preferred_element_type=jnp.float32
    )
    grad_keys = jnp.einsum("hqp,qhd->pd", grad_raw, queries, preferred_element_type=jnp.float32)
    grad_pair = jnp.concatenate([grad_keys, grad_values], axis=-1)
    returned = from_behind(grad_pair[:rows], "ctx", -1)
    grad_own = grad_pair[rows:] + returned
    grad_keyval = jnp.concatenate(
        [rotate_back(grad_own[:, :HD], cosine, sine), grad_own[:, HD:]], axis=-1
    ).astype(jnp.bfloat16)
    grad_query_lin = (
        rotate_back(grad_queries, cosine[:, None, :], sine[:, None, :])
        .reshape(rows, -1)
        .astype(jnp.bfloat16)
    )
    keyval_flat = keyval_w.reshape(width, -1)
    attn_back_part = contract_cols(grad_query_lin, query_w) + contract_cols(
        grad_keyval, keyval_flat
    )
    grad_normed = lax.psum(attn_back_part, "tensor")
    attn_scale = rms_scale(tokens)
    weighted_attn = grad_normed * attn_gain.astype(jnp.float32)
    grad_tokens = (
        grad_middle
        + attn_scale * weighted_attn
        - tokens * attn_scale**3 * jnp.mean(weighted_attn * tokens, axis=-1, keepdims=True)
    )
    updates = (
        contract_rows(normed, grad_query_lin),
        contract_rows(normed, grad_keyval).reshape(keyval_w.shape),
        contract_rows(seed_part_low, context),
        contract_rows(normed_mlp, grad_gateup).reshape(gateup_w.shape),
        contract_rows(mlp_seed, hidden),
        jnp.sum(grad_normed * tokens * attn_scale, axis=0),
        jnp.sum(grad_normed_mlp * middle * mlp_scale, axis=0),
    )
    totals = tuple((running + extra for running, extra in zip(totals, updates)))
    return (totals, grad_tokens.astype(jnp.bfloat16))


def body(
    hidden_in,
    lengths,
    w_query,
    w_keyval,
    w_output,
    w_gateup,
    w_down,
    gain_attn,
    gain_mlp,
    cotangent,
):
    micro, rows, width = hidden_in.shape
    positions = lax.axis_index("ctx") * rows + jnp.arange(rows, dtype=jnp.int32)
    key_positions = jnp.concatenate([positions - rows, positions])
    cosine, sine = rope_tables(positions, HD)
    slot_lengths = lax.dynamic_slice_in_dim(lengths, lax.axis_index("dp") * micro, micro)
    shards = (w_query, w_keyval, w_output, w_gateup, w_down, gain_attn, gain_mlp)

    def forward_fn(squares, packed):
        fresh = (
            lax.all_gather(w_query, ("dp", "ctx"), axis=0, tiled=True),
            lax.all_gather(w_keyval, ("dp", "ctx"), axis=0, tiled=True),
            lax.all_gather(w_output, ("dp", "ctx"), axis=0, tiled=True),
            lax.all_gather(w_gateup, ("dp", "ctx"), axis=0, tiled=True),
            lax.all_gather(w_down, ("dp", "ctx"), axis=0, tiled=True),
            lax.all_gather(gain_attn, ("dp", "ctx"), axis=0, tiled=True),
            lax.all_gather(gain_mlp, ("dp", "ctx"), axis=0, tiled=True),
        )
        return forward_step(fresh, positions, key_positions, cosine, sine, squares, packed)

    def backward_fn(totals, packed):
        fresh = (
            lax.all_gather(w_query, ("dp", "ctx"), axis=0, tiled=True),
            lax.all_gather(w_keyval, ("dp", "ctx"), axis=0, tiled=True),
            lax.all_gather(w_output, ("dp", "ctx"), axis=0, tiled=True),
            lax.all_gather(w_gateup, ("dp", "ctx"), axis=0, tiled=True),
            lax.all_gather(w_down, ("dp", "ctx"), axis=0, tiled=True),
            lax.all_gather(gain_attn, ("dp", "ctx"), axis=0, tiled=True),
            lax.all_gather(gain_mlp, ("dp", "ctx"), axis=0, tiled=True),
        )
        return backward_step(fresh, positions, key_positions, cosine, sine, totals, packed)

    squares, (results, saved) = lax.scan(
        forward_fn, jnp.zeros((3,), jnp.float32), (hidden_in, slot_lengths)
    )
    empty_totals = tuple((jnp.zeros((D,) + shard.shape[1:], jnp.float32) for shard in shards))
    totals, grad_rows = lax.scan(
        backward_fn, empty_totals, (hidden_in, cotangent, slot_lengths, saved)
    )
    square_totals = lax.psum(squares, ("dp", "ctx"))
    valid_count = jnp.sum(lengths).astype(jnp.float32) * D
    root_means = jnp.sqrt(square_totals / valid_count)
    reduced = (
        lax.psum_scatter(totals[0], ("dp", "ctx"), scatter_dimension=0, tiled=True),
        lax.psum_scatter(totals[1], ("dp", "ctx"), scatter_dimension=0, tiled=True),
        lax.psum_scatter(totals[2], ("dp", "ctx"), scatter_dimension=0, tiled=True),
        lax.psum_scatter(totals[3], ("dp", "ctx"), scatter_dimension=0, tiled=True),
        lax.psum_scatter(totals[4], ("dp", "ctx"), scatter_dimension=0, tiled=True),
        lax.psum_scatter(totals[5], ("dp", "ctx"), scatter_dimension=0, tiled=True),
        lax.psum_scatter(totals[6], ("dp", "ctx"), scatter_dimension=0, tiled=True),
    )
    return (
        results,
        grad_rows,
        reduced[0],
        reduced[1],
        reduced[2],
        reduced[3],
        reduced[4],
        reduced[5],
        reduced[6],
        root_means,
    )


def solution(mesh):
    placed = (
        P("dp", "ctx", None),
        P(),
        P(("dp", "ctx"), "tensor"),
        P(("dp", "ctx"), "tensor", None),
        P(("dp", "ctx"), "tensor"),
        P(("dp", "ctx"), None, "tensor"),
        P(("dp", "ctx"), "tensor"),
        P(("dp", "ctx")),
        P(("dp", "ctx")),
        P("dp", "ctx", None),
    )
    return jax.shard_map(
        body,
        mesh=mesh,
        in_specs=placed,
        out_specs=(
            P("dp", "ctx", None),
            P("dp", "ctx", None),
            P(("dp", "ctx"), "tensor"),
            P(("dp", "ctx"), "tensor", None),
            P(("dp", "ctx"), "tensor"),
            P(("dp", "ctx"), None, "tensor"),
            P(("dp", "ctx"), "tensor"),
            P(("dp", "ctx")),
            P(("dp", "ctx")),
            P(),
        ),
        check_vma=False,
    )
```

profile of v0, /device:TPU:0, one launch (start us, length us, event | category | flops | bytes accessed | tf_op | source)
XLA Modules:
  0.0 2640.3 jit_solution(12595167485632672327)
XLA Ops:
  20.6 915.7 %while.54 = (s32[]{:T(128)}, f32[3]{0:T(128)S(1)}, bf16[2,512,2048]{2,1,0:T(8,128)(2,1)}, bf16[2,512,2048]{2,1,0:T(8,128)(2,1)}, bf16[2,512,8,64]{1,3,2,0:T(8,12...) while((s32[]{:T(128)}, f32[3]{0:T(128)S(1)}, ...), condition=%wide.region_10.11_spmd.clone, body=%wide.region_0.10_spmd.clone.sunk | while | flops 12453074944 | bytes 434036544 | solution.py:245
  22.1 14.2 all-gather.12
  38.3 19.8 all_gather.63
  103.7 13.9 all-gather.13
  117.7 140.5 %all-reduce.12.cloned.1.call-done = f32[512,2048]{1,0:T(8,128)} async-done(((f32[512,2048]{1,0:T(8,128)}), f32[512,2048]{1,0:T(8,128)}) %all-reduce.12.cloned.1.call-update) | async-done | bytes 4194320 | tf_op jit(solution)/shard_map/while/body/eval_jaxpr/psum | solution.py:93
  266.8 59.9 %all-gather.31.cloned.1.call-done = bf16[2048,2,1408]{2,1,0:T(2,128)(2,1)} async-done(((bf16[256,2,1408]{2,1,0:T(2,128)(2,1)}), bf16[2048,2,1408]{2,1,0:T(2,128)(2,1)}) %all-gather.31.cloned.1.call-update) | async-done | bytes 11534352 | tf_op jit(solution)/shard_map/while/body/eval_jaxpr/all_gather | solution.py:226
  350.2 12.8 fusion.236
  402.2 65.4 %all-reduce.14.cloned.1.call-done = bf16[512,2048]{1,0:T(8,128)(2,1)} async-done(((bf16[512,2048]{1,0:T(8,128)(2,1)}), bf16[512,2048]{1,0:T(8,128)(2,1)}) %all-reduce.14.cloned.1.call-update) | async-done | bytes 2097168 | tf_op jit(solution)/shard_map/while/body/eval_jaxpr/psum | solution.py:101
  481.4 13.0 all-gather.12
  496.5 18.0 all_gather.63
  560.9 14.6 all-gather.13
  575.6 138.7 %all-reduce.12.cloned.1.call-done = f32[512,2048]{1,0:T(8,128)} async-done(((f32[512,2048]{1,0:T(8,128)}), f32[512,2048]{1,0:T(8,128)}) %all-reduce.12.cloned.1.call-update) | async-done | bytes 4194320 | tf_op jit(solution)/shard_map/while/body/eval_jaxpr/psum | solution.py:93
  722.9 59.9 %all-gather.31.cloned.1.call-done = bf16[2048,2,1408]{2,1,0:T(2,128)(2,1)} async-done(((bf16[256,2,1408]{2,1,0:T(2,128)(2,1)}), bf16[2048,2,1408]{2,1,0:T(2,128)(2,1)}) %all-gather.31.cloned.1.call-update) | async-done | bytes 11534352 | tf_op jit(solution)/shard_map/while/body/eval_jaxpr/all_gather | solution.py:226
  806.4 12.8 fusion.236
  858.5 65.3 %all-reduce.14.cloned.1.call-done = bf16[512,2048]{1,0:T(8,128)(2,1)} async-done(((bf16[512,2048]{1,0:T(8,128)(2,1)}), bf16[512,2048]{1,0:T(8,128)(2,1)}) %all-reduce.14.cloned.1.call-update) | async-done | bytes 2097168 | tf_op jit(solution)/shard_map/while/body/eval_jaxpr/psum | solution.py:101
  938.8 1127.0 %while.55 = (s32[]{:T(128)}, f32[2048,512]{1,0:T(8,128)}, f32[2048,1,128]{2,0,1:T(8,128)}, f32[2048,512]{1,0:T(8,128)}, f32[2048,2,1408]{2,0,1:T(8,128)}, /*inde...) while((s32[]{:T(128)}, f32[2048,512]{1,0:T(8,128)}, ...), condition=%wide.region_21.22_spmd.clone, body=%wide.region_11.21_spmd.clone.sunk | while | flops 25381644288 | bytes 722071680 | solution.py:249
  955.7 35.1 %all-gather.37.cloned.1.call-done = bf16[2048,1408]{1,0:T(8,128)(2,1)} async-done(((bf16[256,1408]{1,0:T(8,128)(2,1)}), bf16[2048,1408]{1,0:T(8,128)(2,1)}) %all-gather.37.cloned.1.call-update) | async-done | bytes 5767184 | tf_op jit(solution)/shard_map/while/body/eval_jaxpr/all_gather | solution.py:239
  1001.0 60.0 %all-gather.35.cloned.1.call-done = bf16[2048,2,1408]{2,0,1:T(8,128)(2,1)} async-done(((bf16[256,2,1408]{2,0,1:T(8,128)(2,1)}), bf16[2048,2,1408]{2,0,1:T(8,128)(2,1)}) %all-gather.35.cloned.1.call-update) | async-done | bytes 11534352 | tf_op jit(solution)/shard_map/while/body/eval_jaxpr/all_gather | solution.py:238
  1061.0 10.8 convolution_bitcast_fusion.3
  1076.4 13.6 all-gather.14
  1090.0 18.4 all_gather.71
  1117.4 109.6 %all-reduce.16.cloned.1.call-done = f32[512,2048]{1,0:T(8,128)} async-done(((f32[512,2048]{1,0:T(8,128)}), f32[512,2048]{1,0:T(8,128)}) %all-reduce.16.cloned.1.call-update) | async-done | bytes 4194320 | tf_op jit(solution)/shard_map/while/body/eval_jaxpr/psum | solution.py:135
  1237.6 18.1 all-gather.33.cloned.1.call-done
  1268.1 22.3 fusion.269
  1300.7 26.5 %broadcast_multiply_fusion.8 = (f32[512,8,64]{0,2,1:T(8,128)}, f32[512,8,64]{0,2,1:T(8,128)}) fusion(f32[512,64]{0,1:T(8,128)} %copy-done.17, f32[8,512,1024]{1,2,0:T(8,128)} %fusion.260, f32[1024,512,8]{1,0,2:T(8,128)} %fusion.265, bf16[1024,128]{0,1:T(8,128)(2,1)S(1)} %dynamic-slice_bitcast_fusion.5), kind=kOutput, calls=%fused_computation.172.clone.1 | convolution fusion | flops 558109696 | bytes 69468160 | tf_op jit(solution)/shard_map/while/body/eval_jaxpr/hqp,pd->qhd/dot_general | solution.py:162
  1336.9 11.4 select_add_fusion.15
  1348.3 14.8 all-gather.15
  1370.6 13.1 select_add_fusion.14
  1394.4 99.7 %all-reduce.18.cloned.1.call-done = f32[512,2048]{1,0:T(8,128)} async-done(((f32[512,2048]{1,0:T(8,128)}), f32[512,2048]{1,0:T(8,128)}) %all-reduce.18.cloned.1.call-update) | async-done | bytes 4194320 | tf_op jit(solution)/shard_map/while/body/eval_jaxpr/psum | solution.py:181
  1514.2 35.1 %all-gather.37.cloned.1.call-done = bf16[2048,1408]{1,0:T(8,128)(2,1)} async-done(((bf16[256,1408]{1,0:T(8,128)(2,1)}), bf16[2048,1408]{1,0:T(8,128)(2,1)}) %all-gather.37.cloned.1.call-update) | async-done | bytes 5767184 | tf_op jit(solution)/shard_map/while/body/eval_jaxpr/all_gather | solution.py:239
  1559.5 60.0 %all-gather.35.cloned.1.call-done = bf16[2048,2,1408]{2,0,1:T(8,128)(2,1)} async-done(((bf16[256,2,1408]{2,0,1:T(8,128)(2,1)}), bf16[2048,2,1408]{2,0,1:T(8,128)(2,1)}) %all-gather.35.cloned.1.call-update) | async-done | bytes 11534352 | tf_op jit(solution)/shard_map/while/body/eval_jaxpr/all_gather | solution.py:238
  1635.3 13.6 all-gather.14
  1648.9 18.5 all_gather.71
  1676.5 109.1 %all-reduce.16.cloned.1.call-done = f32[512,2048]{1,0:T(8,128)} async-done(((f32[512,2048]{1,0:T(8,128)}), f32[512,2048]{1,0:T(8,128)}) %all-reduce.16.cloned.1.call-update) | async-done | bytes 4194320 | tf_op jit(solution)/shard_map/while/body/eval_jaxpr/psum | solution.py:135
  1796.2 18.3 all-gather.33.cloned.1.call-done
  1826.8 22.3 fusion.269
  1859.2 26.5 %broadcast_multiply_fusion.8 = (f32[512,8,64]{0,2,1:T(8,128)}, f32[512,8,64]{0,2,1:T(8,128)}) fusion(f32[512,64]{0,1:T(8,128)} %copy-done.17, f32[8,512,1024]{1,2,0:T(8,128)} %fusion.260, f32[1024,512,8]{1,0,2:T(8,128)} %fusion.265, bf16[1024,128]{0,1:T(8,128)(2,1)S(1)} %dynamic-slice_bitcast_fusion.5), kind=kOutput, calls=%fused_computation.172.clone.1 | convolution fusion | flops 558109696 | bytes 69468160 | tf_op jit(solution)/shard_map/while/body/eval_jaxpr/hqp,pd->qhd/dot_general | solution.py:162
  1895.4 14.5 select_add_fusion.15
  1909.8 15.1 all-gather.15
  1932.4 16.7 select_add_fusion.14
  1960.9 91.7 %all-reduce.18.cloned.1.call-done = f32[512,2048]{1,0:T(8,128)} async-done(((f32[512,2048]{1,0:T(8,128)}), f32[512,2048]{1,0:T(8,128)}) %all-reduce.18.cloned.1.call-update) | async-done | bytes 4194320 | tf_op jit(solution)/shard_map/while/body/eval_jaxpr/psum | solution.py:181
  2065.9 38.7 %copy.57 = f32[2048,2,1408]{2,1,0:T(2,128)} copy(f32[2048,2,1408]{2,0,1:T(8,128)} %get-tuple-element.318) | data formatting | bytes 46137344 | tf_op jit(solution)/shard_map/while | solution.py:249
  2109.9 26.0 all-reduce.3
  2137.6 252.9 %all-reduce.10.cloned.1.call-done = f32[2048,2,1408]{2,1,0:T(2,128)} async-done(((f32[2048,2,1408]{2,1,0:T(2,128)}), f32[2048,2,1408]{2,1,0:T(2,128)}) %all-reduce.10.cloned.1.call-update) | async-done | bytes 23068688
  2394.9 35.5 %reduce-scatter.7.cloned.1.call-done = f32[256,1,128]{2,1,0:T(1,128)} async-done(((f32[2048,1,128]{2,1,0:T(1,128)}), f32[256,1,128]{2,1,0:T(1,128)}) %reduce-scatter.7.cloned.1.call-update) | async-done | bytes 131088 | tf_op jit(solution)/shard_map/reduce_scatter | solution.py:257
  2430.4 55.4 %reduce-scatter.5.cloned.1.call-done = f32[256,512]{1,0:T(8,128)} async-done(((f32[2048,512]{1,0:T(8,128)}), f32[256,512]{1,0:T(8,128)}) %reduce-scatter.5.cloned.1.call-update) | async-done | bytes 524304 | tf_op jit(solution)/shard_map/reduce_scatter | solution.py:256
  2485.8 55.2 %reduce-scatter.9.cloned.1.call-done = f32[256,512]{1,0:T(8,128)} async-done(((f32[2048,512]{1,0:T(8,128)}), f32[256,512]{1,0:T(8,128)}) %reduce-scatter.9.cloned.1.call-update) | async-done | bytes 524304 | tf_op jit(solution)/shard_map/reduce_scatter | solution.py:258
  2541.0 91.1 %reduce-scatter.11.cloned.1.call-done = f32[256,1408]{1,0:T(8,128)} async-done(((f32[2048,1408]{1,0:T(8,128)}), f32[256,1408]{1,0:T(8,128)}) %reduce-scatter.11.cloned.1.call-update) | async-done | bytes 1441808 | tf_op jit(solution)/shard_map/reduce_scatter | solution.py:260
  (458 shorter events, 511.9 us)
Async XLA Ops:
  20.6 46.2 %all-gather.25.cloned.1.call-start = ((), (), s32[]{:S(2)}) async-start(), calls=%async_computation.9 | async-start | bytes 2359296 | tf_op jit(solution)/shard_map/while/body/eval_jaxpr/all_gather | solution.py:223
  21.4 75.5 %all-gather.27.cloned.1.call-start = ((), (), s32[]{:S(2)}) async-start(), calls=%async_computation.10 | async-start | bytes 2359296 | tf_op jit(solution)/shard_map/while/body/eval_jaxpr/all_gather | solution.py:225
  60.8 6.0 collective-permute-start
  63.2 195.0 %all-reduce.12.cloned.1.call-start = ((), (), s32[]{:S(2)}) async-start(), calls=%async_computation.11 | async-start | bytes 8388608 | tf_op jit(solution)/shard_map/while/body/eval_jaxpr/psum | solution.py:93
  101.8 224.8 %all-gather.31.cloned.1.call-start = ((), (), s32[]{:S(2)}) async-start(), calls=%async_computation.13 | async-start | bytes 12976128 | tf_op jit(solution)/shard_map/while/body/eval_jaxpr/all_gather | solution.py:226
  102.4 269.3 %all-gather.29.cloned.1.call-start = ((), (), s32[]{:S(2)}) async-start(), calls=%async_computation.12 | async-start | bytes 6488064 | tf_op jit(solution)/shard_map/while/body/eval_jaxpr/all_gather | solution.py:227
  103.0 364.6 %all-reduce.14.cloned.1.call-start = ((), (), s32[]{:S(2)}) async-start(), calls=%async_computation.14 | async-start | bytes 4194304 | tf_op jit(solution)/shard_map/while/body/eval_jaxpr/psum | solution.py:101
  480.0 43.8 %all-gather.25.cloned.1.call-start = ((), (), s32[]{:S(2)}) async-start(), calls=%async_computation.9 | async-start | bytes 2359296 | tf_op jit(solution)/shard_map/while/body/eval_jaxpr/all_gather | solution.py:223
  480.7 73.2 %all-gather.27.cloned.1.call-start = ((), (), s32[]{:S(2)}) async-start(), calls=%async_computation.10 | async-start | bytes 2359296 | tf_op jit(solution)/shard_map/while/body/eval_jaxpr/all_gather | solution.py:225
  517.1 6.7 collective-permute-start
  520.7 193.6 %all-reduce.12.cloned.1.call-start = ((), (), s32[]{:S(2)}) async-start(), calls=%async_computation.11 | async-start | bytes 8388608 | tf_op jit(solution)/shard_map/while/body/eval_jaxpr/psum | solution.py:93
  558.9 223.9 %all-gather.31.cloned.1.call-start = ((), (), s32[]{:S(2)}) async-start(), calls=%async_computation.13 | async-start | bytes 12976128 | tf_op jit(solution)/shard_map/while/body/eval_jaxpr/all_gather | solution.py:226
  559.5 268.5 %all-gather.29.cloned.1.call-start = ((), (), s32[]{:S(2)}) async-start(), calls=%async_computation.12 | async-start | bytes 6488064 | tf_op jit(solution)/shard_map/while/body/eval_jaxpr/all_gather | solution.py:227
  560.2 363.6 %all-reduce.14.cloned.1.call-start = ((), (), s32[]{:S(2)}) async-start(), calls=%async_computation.14 | async-start | bytes 4194304 | tf_op jit(solution)/shard_map/while/body/eval_jaxpr/psum | solution.py:101
  945.6 388.4 %copy-start.10 = (f32[512,64]{0,1:T(8,128)}, f32[512,64]{0,1:T(8,128)S(1)}, u32[]{:S(2)}) copy-start(f32[512,64]{0,1:T(8,128)S(1)} %get-tuple-element.1391) | copy-start | bytes 393220 | tf_op jit(solution)/shard_map/while
  945.6 45.2 %all-gather.37.cloned.1.call-start = ((), (), s32[]{:S(2)}) async-start(), calls=%async_computation.17 | async-start | bytes 6488064 | tf_op jit(solution)/shard_map/while/body/eval_jaxpr/all_gather | solution.py:239
  946.3 114.6 %all-gather.35.cloned.1.call-start = ((), (), s32[]{:S(2)}) async-start(), calls=%async_computation.16 | async-start | bytes 12976128 | tf_op jit(solution)/shard_map/while/body/eval_jaxpr/all_gather | solution.py:238
  946.9 280.1 %all-reduce.16.cloned.1.call-start = ((), (), s32[]{:S(2)}) async-start(), calls=%async_computation.18 | async-start | bytes 8388608 | tf_op jit(solution)/shard_map/while/body/eval_jaxpr/psum | solution.py:135
  1001.0 70.9 %copy-start.16 = (bf16[512,1,1408]{2,0,1:T(8,128)(2,1)}, bf16[512,1,1408]{2,0,1:T(8,128)(2,1)S(1)}, u32[]{:S(2)}) copy-start(bf16[512,1,1408]{2,0,1:T(8,128)(2,1)S(1)} %get-tuple-element.1210) | copy-start | bytes 4325380 | tf_op jit(solution)/shard_map/while
  1071.9 37.4 %copy-start.41 = (bf16[2,512,8,64]{1,3,2,0:T(8,128)(2,1)S(1)}, bf16[2,512,8,64]{1,3,2,0:T(8,128)(2,1)}, u32[]{:S(2)}) copy-start(bf16[2,512,8,64]{1,3,2,0:T(8,128)(2,1)} %get-tuple-element.1382) | copy-start | bytes 3145732 | tf_op jit(solution)/shard_map/while
  1071.9 183.8 %all-gather.33.cloned.1.call-start = ((), (), s32[]{:S(2)}) async-start(), calls=%async_computation.15 | async-start | bytes 2359296 | tf_op jit(solution)/shard_map/while/body/eval_jaxpr/all_gather | solution.py:237
  1072.5 257.5 %all-gather.39.cloned.1.call-start = ((), (), s32[]{:S(2)}) async-start(), calls=%async_computation.19 | async-start | bytes 2359296 | tf_op jit(solution)/shard_map/while/body/eval_jaxpr/all_gather | solution.py:235
  1073.1 421.0 %all-reduce.18.cloned.1.call-start = ((), (), s32[]{:S(2)}) async-start(), calls=%async_computation.20 | async-start | bytes 8388608 | tf_op jit(solution)/shard_map/while/body/eval_jaxpr/psum | solution.py:181
  1299.0 34.0 %collective-permute-start.1 = (f32[512,128]{0,1:T(8,128)S(1)}, f32[512,128]{0,1:T(8,128)S(1)}, u32[]{:S(2)}, u32[]{:S(2)}) collective-permute-start(f32[512,128]{0,1:T(8,128)S(1)} %pad_maximum_fusion.13), channel_id=1, source_target_pairs={{4,0},{5,1},{6,2},{7,3},{12,8},{13,9},{14,10},{15,11},{20,16},{21,... | collective-permute-start | bytes 786440 | tf_op jit(solution)/shard_map/while/body/eval_jaxpr/ppermute | solution.py:16
  1393.3 100.8 %copy-start.30 = (f32[512]{0:T(512)S(1)}, f32[512]{0:T(512)}, u32[]{:S(2)}) copy-start(f32[512]{0:T(512)} %get-tuple-element.1220) | copy-start | bytes 6148 | tf_op jit(solution)/shard_map/while
  1394.4 109.4 %copy-start.15 = (f32[2048,1,128]{2,0,1:T(8,128)}, f32[2048,1,128]{2,0,1:T(8,128)S(1)}, u32[]{:S(2)}) copy-start(f32[2048,1,128]{2,0,1:T(8,128)S(1)} %fusion.273) | copy-start | bytes 3145732 | tf_op jit(solution)/shard_map/while
  1394.4 104.0 %copy-start.34 = (f32[2048]{0:T(1024)S(1)}, f32[2048]{0:T(1024)}, u32[]{:S(2)}) copy-start(f32[2048]{0:T(1024)} %get-tuple-element.1342) | copy-start | bytes 24580 | tf_op jit(solution)/shard_map/while
  1394.4 104.0 %copy-start.37 = (f32[512]{0:T(512)S(1)}, f32[512]{0:T(512)}, u32[]{:S(2)}) copy-start(f32[512]{0:T(512)} %get-tuple-element.1224) | copy-start | bytes 6148 | tf_op jit(solution)/shard_map/while
  1504.1 388.4 %copy-start.10 = (f32[512,64]{0,1:T(8,128)}, f32[512,64]{0,1:T(8,128)S(1)}, u32[]{:S(2)}) copy-start(f32[512,64]{0,1:T(8,128)S(1)} %get-tuple-element.1391) | copy-start | bytes 393220 | tf_op jit(solution)/shard_map/while
  1504.1 45.2 %all-gather.37.cloned.1.call-start = ((), (), s32[]{:S(2)}) async-start(), calls=%async_computation.17 | async-start | bytes 6488064 | tf_op jit(solution)/shard_map/while/body/eval_jaxpr/all_gather | solution.py:239
  1504.9 114.7 %all-gather.35.cloned.1.call-start = ((), (), s32[]{:S(2)}) async-start(), calls=%async_computation.16 | async-start | bytes 12976128 | tf_op jit(solution)/shard_map/while/body/eval_jaxpr/all_gather | solution.py:238
  1505.5 280.1 %all-reduce.16.cloned.1.call-start = ((), (), s32[]{:S(2)}) async-start(), calls=%async_computation.18 | async-start | bytes 8388608 | tf_op jit(solution)/shard_map/while/body/eval_jaxpr/psum | solution.py:135
  1559.5 70.9 %copy-start.16 = (bf16[512,1,1408]{2,0,1:T(8,128)(2,1)}, bf16[512,1,1408]{2,0,1:T(8,128)(2,1)S(1)}, u32[]{:S(2)}) copy-start(bf16[512,1,1408]{2,0,1:T(8,128)(2,1)S(1)} %get-tuple-element.1210) | copy-start | bytes 4325380 | tf_op jit(solution)/shard_map/while
  1630.4 18.5 copy-start.24
  1630.5 37.9 %copy-start.41 = (bf16[2,512,8,64]{1,3,2,0:T(8,128)(2,1)S(1)}, bf16[2,512,8,64]{1,3,2,0:T(8,128)(2,1)}, u32[]{:S(2)}) copy-start(bf16[2,512,8,64]{1,3,2,0:T(8,128)(2,1)} %get-tuple-element.1382) | copy-start | bytes 3145732 | tf_op jit(solution)/shard_map/while
  1630.5 184.0 %all-gather.33.cloned.1.call-start = ((), (), s32[]{:S(2)}) async-start(), calls=%async_computation.15 | async-start | bytes 2359296 | tf_op jit(solution)/shard_map/while/body/eval_jaxpr/all_gather | solution.py:237
  1631.2 257.3 %all-gather.39.cloned.1.call-start = ((), (), s32[]{:S(2)}) async-start(), calls=%async_computation.19 | async-start | bytes 2359296 | tf_op jit(solution)/shard_map/while/body/eval_jaxpr/all_gather | solution.py:235
  1632.0 420.6 %all-reduce.18.cloned.1.call-start = ((), (), s32[]{:S(2)}) async-start(), calls=%async_computation.20 | async-start | bytes 8388608 | tf_op jit(solution)/shard_map/while/body/eval_jaxpr/psum | solution.py:181
  1857.7 33.8 %collective-permute-start.1 = (f32[512,128]{0,1:T(8,128)S(1)}, f32[512,128]{0,1:T(8,128)S(1)}, u32[]{:S(2)}, u32[]{:S(2)}) collective-permute-start(f32[512,128]{0,1:T(8,128)S(1)} %pad_maximum_fusion.13), channel_id=1, source_target_pairs={{4,0},{5,1},{6,2},{7,3},{12,8},{13,9},{14,10},{15,11},{20,16},{21,... | collective-permute-start | bytes 786440 | tf_op jit(solution)/shard_map/while/body/eval_jaxpr/ppermute | solution.py:16
  1959.8 92.8 %copy-start.30 = (f32[512]{0:T(512)S(1)}, f32[512]{0:T(512)}, u32[]{:S(2)}) copy-start(f32[512]{0:T(512)} %get-tuple-element.1220) | copy-start | bytes 6148 | tf_op jit(solution)/shard_map/while
  1960.8 101.5 %copy-start.15 = (f32[2048,1,128]{2,0,1:T(8,128)}, f32[2048,1,128]{2,0,1:T(8,128)S(1)}, u32[]{:S(2)}) copy-start(f32[2048,1,128]{2,0,1:T(8,128)S(1)} %fusion.273) | copy-start | bytes 3145732 | tf_op jit(solution)/shard_map/while
  1960.9 96.0 %copy-start.34 = (f32[2048]{0:T(1024)S(1)}, f32[2048]{0:T(1024)}, u32[]{:S(2)}) copy-start(f32[2048]{0:T(1024)} %get-tuple-element.1342) | copy-start | bytes 24580 | tf_op jit(solution)/shard_map/while
  1960.9 96.0 %copy-start.37 = (f32[512]{0:T(512)S(1)}, f32[512]{0:T(512)}, u32[]{:S(2)}) copy-start(f32[512]{0:T(512)} %get-tuple-element.1224) | copy-start | bytes 6148 | tf_op jit(solution)/shard_map/while
  2065.9 324.7 %all-reduce.10.cloned.1.call-start = ((), (), s32[]{:S(2)}) async-start(), calls=%async_computation.8 | async-start | bytes 46137344
  2104.6 325.8 %reduce-scatter.7.cloned.1.call-start = ((), (), s32[]{:S(2)}) async-start(), calls=%async_computation.5 | async-start | bytes 1179648 | tf_op jit(solution)/shard_map/reduce_scatter | solution.py:257
  2105.2 380.6 %reduce-scatter.5.cloned.1.call-start = ((), (), s32[]{:S(2)}) async-start(), calls=%async_computation.4 | async-start | bytes 4718592 | tf_op jit(solution)/shard_map/reduce_scatter | solution.py:256
  2105.8 435.2 %reduce-scatter.9.cloned.1.call-start = ((), (), s32[]{:S(2)}) async-start(), calls=%async_computation.6 | async-start | bytes 4718592 | tf_op jit(solution)/shard_map/reduce_scatter | solution.py:258
  2106.5 525.6 %reduce-scatter.11.cloned.1.call-start = ((), (), s32[]{:S(2)}) async-start(), calls=%async_computation.7 | async-start | bytes 12976128 | tf_op jit(solution)/shard_map/reduce_scatter | solution.py:260
  (75 other events, 465.2 us)
Sparse Core Ops, SparseCore 0:
  24.1 32.3 all-gather.24
  63.3 27.7 all-gather.26
  101.9 156.1 all-reduce.11
  259.9 66.6 all-gather.30
  328.4 43.3 all-gather.28
  381.0 86.4 all-reduce.13
  483.4 27.5 all-gather.24
  520.8 26.1 all-gather.26
  559.0 155.2 all-reduce.11
  716.0 66.6 all-gather.30
  784.6 43.3 all-gather.28
  837.3 86.4 all-reduce.13
  948.5 42.2 all-gather.36
  993.3 67.6 all-gather.34
  1072.0 154.9 all-reduce.15
  1228.8 26.8 all-gather.32
  1257.4 27.9 all-gather.38
  1337.0 157.0 all-reduce.17
  1507.0 42.3 all-gather.36
  1551.8 67.6 all-gather.34
  1630.6 154.9 all-reduce.15
  1787.5 26.8 all-gather.32
  1816.3 27.9 all-gather.38
  1895.5 157.0 all-reduce.17
Sparse Core Ops, SparseCore 1:
  2104.7 285.7 all-reduce.9
  2394.5 35.9 reduce-scatter.6
  2434.6 51.2 reduce-scatter.4
  2489.8 51.2 reduce-scatter.8
  2545.5 86.6 reduce-scatter.10
where the time goes:
time: 2660 us; the launch traced here: 2640 us
  waiting for transfers between devices  1690 us (64%)
  matrix products  371 us (14%)
  blocking collectives  213 us (8%)
  local copies, waits for them, and re-layouts  190 us (7%)
  other arithmetic  140 us (5%)
    psum x2, waiting for transfers between devices, forward_step(): attn_out = lax.psum(attn_part, 'tensor')  279 us
    unnamed x6, waiting for transfers between devices  255 us
    psum x2, waiting for transfers between devices, backward_step(): grad_normed_mlp = lax.psum(mlp_back_part, 'tensor')  219 us
    psum x2, waiting for transfers between devices, backward_step(): grad_normed = lax.psum(attn_back_part, 'tensor')  191 us
    psum x2, waiting for transfers between devices, forward_step(): lax.psum(mlp_part.astype(jnp.bfloat16), 'tensor').astype(jnp.float32)  131 us
    all_gather x2, waiting for transfers between devices, backward_fn(): lax.all_gather(w_gateup, ('dp', 'ctx'), axis=0, tiled=True)  120 us
    all_gather x2, waiting for transfers between devices, forward_fn(): lax.all_gather(w_gateup, ('dp', 'ctx'), axis=0, tiled=True)  120 us
    reduce_scatter x1, waiting for transfers between devices, body(): lax.psum_scatter(totals[4], ('dp', 'ctx'), scatter_dimension=0, tiled=True)  91.1 us
  transfers between devices with their start and end apart: 33, of which 25 were waited for; matrix products, arithmetic and copies ran while one was open for 20% of the time, Pallas kernels for 0%

commit v1 on v0

--- a/solution.py
+++ b/solution.py
@@ -178,7 +178,11 @@
     attn_back_part = contract_cols(grad_query_lin, query_w) + contract_cols(
         grad_keyval, keyval_flat
     )
-    grad_normed = lax.psum(attn_back_part, "tensor")
+    grad_normed = attn_back_part
+    for hop in (1, 2):
+        grad_normed = grad_normed + lax.ppermute(
+            grad_normed, "tensor", [(dev, dev ^ hop) for dev in range(4)]
+        )
     attn_scale = rms_scale(tokens)
     weighted_attn = grad_normed * attn_gain.astype(jnp.float32)
     grad_tokens = (

time: 2660 us -> 2920 us (1.098)
  waiting for transfers between devices: 1690 us -> 1940 us
    ppermute x0 -> x4, waiting for transfers between devices: none -> 438 us  [backward_step(): lax.ppermute(grad_normed, 'tensor', [(dev, dev ^ hop) for dev in range(4)])]
    psum x2 -> x0, waiting for transfers between devices: 191 us -> none  [backward_step(): grad_normed = lax.psum(attn_back_part, 'tensor')]
  transfers between devices with their start and end apart: 33 -> 35, of which waited for: 25 -> 27; matrix products, arithmetic and copies ran while one was open for 20% -> 18% of each run, Pallas kernels for 0% -> 0%
where the time goes in v1:
time: 2920 us; the launch traced here: 2900 us
  waiting for transfers between devices  1940 us (66%)
  matrix products  361 us (12%)
  blocking collectives  211 us (7%)
  local copies, waits for them, and re-layouts  190 us (7%)
  other arithmetic  152 us (5%)
    ppermute x4, waiting for transfers between devices, backward_step(): lax.ppermute(grad_normed, 'tensor', [(dev, dev ^ hop) for dev in range(4)])  438 us
    psum x2, waiting for transfers between devices, forward_step(): attn_out = lax.psum(attn_part, 'tensor')  279 us
    unnamed x6, waiting for transfers between devices  258 us
    psum x2, waiting for transfers between devices, backward_step(): grad_normed_mlp = lax.psum(mlp_back_part, 'tensor')  219 us
    psum x2, waiting for transfers between devices, forward_step(): lax.psum(mlp_part.astype(jnp.bfloat16), 'tensor').astype(jnp.float32)  131 us
    all_gather x2, waiting for transfers between devices, backward_fn(): lax.all_gather(w_gateup, ('dp', 'ctx'), axis=0, tiled=True)  120 us
    all_gather x2, waiting for transfers between devices, forward_fn(): lax.all_gather(w_gateup, ('dp', 'ctx'), axis=0, tiled=True)  120 us
    reduce_scatter x1, waiting for transfers between devices, body(): lax.psum_scatter(totals[4], ('dp', 'ctx'), scatter_dimension=0, tiled=True)  91.1 us
  transfers between devices with their start and end apart: 35, of which 27 were waited for; matrix products, arithmetic and copies ran while one was open for 18% of the time, Pallas kernels for 0%

profile of v1, /device:TPU:0, one launch (start us, length us, event | category | flops | bytes accessed | tf_op | source)
XLA Modules:
  0.0 2899.4 jit_solution(17960184575818893438)
XLA Ops:
  20.6 915.4 %while.54 = (s32[]{:T(128)}, f32[3]{0:T(128)S(1)}, bf16[2,512,2048]{2,1,0:T(8,128)(2,1)}, bf16[2,512,2048]{2,1,0:T(8,128)(2,1)}, bf16[2,512,8,64]{1,3,2,0:T(8,12...) while((s32[]{:T(128)}, f32[3]{0:T(128)S(1)}, ...), condition=%wide.region_10.11_spmd.clone, body=%wide.region_0.10_spmd.clone.sunk | while | flops 12453074944 | bytes 434036544 | solution.py:249
  22.0 14.2 all-gather.12
  38.3 19.8 all_gather.63
  103.6 14.0 all-gather.13
  117.6 140.5 %all-reduce.11.cloned.1.call-done = f32[512,2048]{1,0:T(8,128)} async-done(((f32[512,2048]{1,0:T(8,128)}), f32[512,2048]{1,0:T(8,128)}) %all-reduce.11.cloned.1.call-update) | async-done | bytes 4194320 | tf_op jit(solution)/shard_map/while/body/eval_jaxpr/psum | solution.py:93
  266.7 59.9 %all-gather.31.cloned.1.call-done = bf16[2048,2,1408]{2,1,0:T(2,128)(2,1)} async-done(((bf16[256,2,1408]{2,1,0:T(2,128)(2,1)}), bf16[2048,2,1408]{2,1,0:T(2,128)(2,1)}) %all-gather.31.cloned.1.call-update) | async-done | bytes 11534352 | tf_op jit(solution)/shard_map/while/body/eval_jaxpr/all_gather | solution.py:230
  350.2 12.7 fusion.236
  402.1 65.4 %all-reduce.13.cloned.1.call-done = bf16[512,2048]{1,0:T(8,128)(2,1)} async-done(((bf16[512,2048]{1,0:T(8,128)(2,1)}), bf16[512,2048]{1,0:T(8,128)(2,1)}) %all-reduce.13.cloned.1.call-update) | async-done | bytes 2097168 | tf_op jit(solution)/shard_map/while/body/eval_jaxpr/psum | solution.py:101
  481.3 13.0 all-gather.12
  496.3 18.0 all_gather.63
  560.8 14.6 all-gather.13
  575.4 138.7 %all-reduce.11.cloned.1.call-done = f32[512,2048]{1,0:T(8,128)} async-done(((f32[512,2048]{1,0:T(8,128)}), f32[512,2048]{1,0:T(8,128)}) %all-reduce.11.cloned.1.call-update) | async-done | bytes 4194320 | tf_op jit(solution)/shard_map/while/body/eval_jaxpr/psum | solution.py:93
  722.7 59.8 %all-gather.31.cloned.1.call-done = bf16[2048,2,1408]{2,1,0:T(2,128)(2,1)} async-done(((bf16[256,2,1408]{2,1,0:T(2,128)(2,1)}), bf16[2048,2,1408]{2,1,0:T(2,128)(2,1)}) %all-gather.31.cloned.1.call-update) | async-done | bytes 11534352 | tf_op jit(solution)/shard_map/while/body/eval_jaxpr/all_gather | solution.py:230
  806.1 12.7 fusion.236
  858.3 65.3 %all-reduce.13.cloned.1.call-done = bf16[512,2048]{1,0:T(8,128)(2,1)} async-done(((bf16[512,2048]{1,0:T(8,128)(2,1)}), bf16[512,2048]{1,0:T(8,128)(2,1)}) %all-reduce.13.cloned.1.call-update) | async-done | bytes 2097168 | tf_op jit(solution)/shard_map/while/body/eval_jaxpr/psum | solution.py:101
  938.5 1384.0 %while.55 = (s32[]{:T(128)}, f32[2048,512]{1,0:T(8,128)}, f32[2048,1,128]{2,0,1:T(8,128)}, f32[2048,512]{1,0:T(8,128)}, f32[2048,2,1408]{2,0,1:T(8,128)}, /*inde...) while((s32[]{:T(128)}, f32[2048,512]{1,0:T(8,128)}, ...), condition=%wide.region_20.21_spmd.clone, body=%wide.region_11.20_spmd.clone.sunk | while | flops 25383741440 | bytes 819064960 | solution.py:253
  955.4 35.1 %all-gather.37.cloned.1.call-done = bf16[2048,1408]{1,0:T(8,128)(2,1)} async-done(((bf16[256,1408]{1,0:T(8,128)(2,1)}), bf16[2048,1408]{1,0:T(8,128)(2,1)}) %all-gather.37.cloned.1.call-update) | async-done | bytes 5767184 | tf_op jit(solution)/shard_map/while/body/eval_jaxpr/all_gather | solution.py:243
  1000.6 60.0 %all-gather.35.cloned.1.call-done = bf16[2048,2,1408]{2,0,1:T(8,128)(2,1)} async-done(((bf16[256,2,1408]{2,0,1:T(8,128)(2,1)}), bf16[2048,2,1408]{2,0,1:T(8,128)(2,1)}) %all-gather.35.cloned.1.call-update) | async-done | bytes 11534352 | tf_op jit(solution)/shard_map/while/body/eval_jaxpr/all_gather | solution.py:242
  1075.9 13.6 all-gather.14
  1089.5 18.3 all_gather.71
  1116.8 109.8 %all-reduce.15.cloned.1.call-done = f32[512,2048]{1,0:T(8,128)} async-done(((f32[512,2048]{1,0:T(8,128)}), f32[512,2048]{1,0:T(8,128)}) %all-reduce.15.cloned.1.call-update) | async-done | bytes 4194320 | tf_op jit(solution)/shard_map/while/body/eval_jaxpr/psum | solution.py:135
  1237.1 18.1 all-gather.33.cloned.1.call-done
  1267.6 22.3 fusion.269
  1300.2 26.7 broadcast_multiply_fusion.8
  1338.1 91.6 %collective-permute-done.2 = f32[512,2048]{1,0:T(8,128)} collective-permute-done((f32[512,2048]{1,0:T(8,128)}, f32[512,2048]{1,0:T(8,128)}, u32[]{:S(2)}, u32[]{:S(2)}) %collective-permute-start.2) | collective-permute-done | bytes 4194336 | tf_op jit(solution)/shard_map/while/body/eval_jaxpr/ppermute | solution.py:183
  1445.3 13.6 all-gather.15
  1466.5 13.1 select_add_fusion.14
  1488.4 130.9 %collective-permute-done.3 = f32[512,2048]{1,0:T(8,128)} collective-permute-done((f32[512,2048]{1,0:T(8,128)}, f32[512,2048]{1,0:T(8,128)}, u32[]{:S(2)}, u32[]{:S(2)}) %collective-permute-start.3) | collective-permute-done | bytes 4194336 | tf_op jit(solution)/shard_map/while/body/eval_jaxpr/ppermute | solution.py:183
  1641.2 37.3 %all-gather.37.cloned.1.call-done = bf16[2048,1408]{1,0:T(8,128)(2,1)} async-done(((bf16[256,1408]{1,0:T(8,128)(2,1)}), bf16[2048,1408]{1,0:T(8,128)(2,1)}) %all-gather.37.cloned.1.call-update) | async-done | bytes 5767184 | tf_op jit(solution)/shard_map/while/body/eval_jaxpr/all_gather | solution.py:243
  1688.7 60.2 %all-gather.35.cloned.1.call-done = bf16[2048,2,1408]{2,0,1:T(8,128)(2,1)} async-done(((bf16[256,2,1408]{2,0,1:T(8,128)(2,1)}), bf16[2048,2,1408]{2,0,1:T(8,128)(2,1)}) %all-gather.35.cloned.1.call-update) | async-done | bytes 11534352 | tf_op jit(solution)/shard_map/while/body/eval_jaxpr/all_gather | solution.py:242
  1748.9 10.7 convolution_bitcast_fusion.3
  1764.4 13.6 all-gather.14
  1778.1 18.5 all_gather.71
  1805.6 109.2 %all-reduce.15.cloned.1.call-done = f32[512,2048]{1,0:T(8,128)} async-done(((f32[512,2048]{1,0:T(8,128)}), f32[512,2048]{1,0:T(8,128)}) %all-reduce.15.cloned.1.call-update) | async-done | bytes 4194320 | tf_op jit(solution)/shard_map/while/body/eval_jaxpr/psum | solution.py:135
  1925.3 18.3 all-gather.33.cloned.1.call-done
  1956.0 22.3 fusion.269
  1988.4 26.7 broadcast_multiply_fusion.8
  2026.2 91.6 %collective-permute-done.2 = f32[512,2048]{1,0:T(8,128)} collective-permute-done((f32[512,2048]{1,0:T(8,128)}, f32[512,2048]{1,0:T(8,128)}, u32[]{:S(2)}, u32[]{:S(2)}) %collective-permute-start.2) | collective-permute-done | bytes 4194336 | tf_op jit(solution)/shard_map/while/body/eval_jaxpr/ppermute | solution.py:183
  2136.1 13.7 all-gather.15
  2157.3 16.5 select_add_fusion.14
  2183.9 123.5 %collective-permute-done.3 = f32[512,2048]{1,0:T(8,128)} collective-permute-done((f32[512,2048]{1,0:T(8,128)}, f32[512,2048]{1,0:T(8,128)}, u32[]{:S(2)}, u32[]{:S(2)}) %collective-permute-start.3) | collective-permute-done | bytes 4194336 | tf_op jit(solution)/shard_map/while/body/eval_jaxpr/ppermute | solution.py:183
  2322.6 38.7 %copy.57 = f32[2048,2,1408]{2,1,0:T(2,128)} copy(f32[2048,2,1408]{2,0,1:T(8,128)} %get-tuple-element.318) | data formatting | bytes 46137344 | tf_op jit(solution)/shard_map/while | solution.py:253
  2366.5 26.0 all-reduce.3
  2394.3 255.4 %all-reduce.9.cloned.1.call-done = f32[2048,2,1408]{2,1,0:T(2,128)} async-done(((f32[2048,2,1408]{2,1,0:T(2,128)}), f32[2048,2,1408]{2,1,0:T(2,128)}) %all-reduce.9.cloned.1.call-update) | async-done | bytes 23068688
  2654.0 35.5 %reduce-scatter.7.cloned.1.call-done = f32[256,1,128]{2,1,0:T(1,128)} async-done(((f32[2048,1,128]{2,1,0:T(1,128)}), f32[256,1,128]{2,1,0:T(1,128)}) %reduce-scatter.7.cloned.1.call-update) | async-done | bytes 131088 | tf_op jit(solution)/shard_map/reduce_scatter | solution.py:261
  2689.5 55.4 %reduce-scatter.5.cloned.1.call-done = f32[256,512]{1,0:T(8,128)} async-done(((f32[2048,512]{1,0:T(8,128)}), f32[256,512]{1,0:T(8,128)}) %reduce-scatter.5.cloned.1.call-update) | async-done | bytes 524304 | tf_op jit(solution)/shard_map/reduce_scatter | solution.py:260
  2744.9 55.2 %reduce-scatter.9.cloned.1.call-done = f32[256,512]{1,0:T(8,128)} async-done(((f32[2048,512]{1,0:T(8,128)}), f32[256,512]{1,0:T(8,128)}) %reduce-scatter.9.cloned.1.call-update) | async-done | bytes 524304 | tf_op jit(solution)/shard_map/reduce_scatter | solution.py:262
  2800.1 91.1 %reduce-scatter.11.cloned.1.call-done = f32[256,1408]{1,0:T(8,128)} async-done(((f32[2048,1408]{1,0:T(8,128)}), f32[256,1408]{1,0:T(8,128)}) %reduce-scatter.11.cloned.1.call-update) | async-done | bytes 1441808 | tf_op jit(solution)/shard_map/reduce_scatter | solution.py:264
  (484 shorter events, 548.3 us)
Async XLA Ops:
  20.6 46.2 %all-gather.25.cloned.1.call-start = ((), (), s32[]{:S(2)}) async-start(), calls=%async_computation.9 | async-start | bytes 2359296 | tf_op jit(solution)/shard_map/while/body/eval_jaxpr/all_gather | solution.py:227
  21.3 75.5 %all-gather.27.cloned.1.call-start = ((), (), s32[]{:S(2)}) async-start(), calls=%async_computation.10 | async-start | bytes 2359296 | tf_op jit(solution)/shard_map/while/body/eval_jaxpr/all_gather | solution.py:229
  60.8 6.0 collective-permute-start
  63.2 194.9 %all-reduce.11.cloned.1.call-start = ((), (), s32[]{:S(2)}) async-start(), calls=%async_computation.11 | async-start | bytes 8388608 | tf_op jit(solution)/shard_map/while/body/eval_jaxpr/psum | solution.py:93
  101.8 224.8 %all-gather.31.cloned.1.call-start = ((), (), s32[]{:S(2)}) async-start(), calls=%async_computation.13 | async-start | bytes 12976128 | tf_op jit(solution)/shard_map/while/body/eval_jaxpr/all_gather | solution.py:230
  102.3 269.3 %all-gather.29.cloned.1.call-start = ((), (), s32[]{:S(2)}) async-start(), calls=%async_computation.12 | async-start | bytes 6488064 | tf_op jit(solution)/shard_map/while/body/eval_jaxpr/all_gather | solution.py:231
  102.9 364.5 %all-reduce.13.cloned.1.call-start = ((), (), s32[]{:S(2)}) async-start(), calls=%async_computation.14 | async-start | bytes 4194304 | tf_op jit(solution)/shard_map/while/body/eval_jaxpr/psum | solution.py:101
  479.8 43.8 %all-gather.25.cloned.1.call-start = ((), (), s32[]{:S(2)}) async-start(), calls=%async_computation.9 | async-start | bytes 2359296 | tf_op jit(solution)/shard_map/while/body/eval_jaxpr/all_gather | solution.py:227
  480.6 73.2 %all-gather.27.cloned.1.call-start = ((), (), s32[]{:S(2)}) async-start(), calls=%async_computation.10 | async-start | bytes 2359296 | tf_op jit(solution)/shard_map/while/body/eval_jaxpr/all_gather | solution.py:229
  517.0 6.7 collective-permute-start
  520.5 193.5 %all-reduce.11.cloned.1.call-start = ((), (), s32[]{:S(2)}) async-start(), calls=%async_computation.11 | async-start | bytes 8388608 | tf_op jit(solution)/shard_map/while/body/eval_jaxpr/psum | solution.py:93
  558.7 223.8 %all-gather.31.cloned.1.call-start = ((), (), s32[]{:S(2)}) async-start(), calls=%async_computation.13 | async-start | bytes 12976128 | tf_op jit(solution)/shard_map/while/body/eval_jaxpr/all_gather | solution.py:230
  559.3 268.5 %all-gather.29.cloned.1.call-start = ((), (), s32[]{:S(2)}) async-start(), calls=%async_computation.12 | async-start | bytes 6488064 | tf_op jit(solution)/shard_map/while/body/eval_jaxpr/all_gather | solution.py:231
  560.0 363.6 %all-reduce.13.cloned.1.call-start = ((), (), s32[]{:S(2)}) async-start(), calls=%async_computation.14 | async-start | bytes 4194304 | tf_op jit(solution)/shard_map/while/body/eval_jaxpr/psum | solution.py:101
  945.2 388.5 %copy-start.10 = (f32[512,64]{0,1:T(8,128)}, f32[512,64]{0,1:T(8,128)S(1)}, u32[]{:S(2)}) copy-start(f32[512,64]{0,1:T(8,128)S(1)} %get-tuple-element.1391) | copy-start | bytes 393220 | tf_op jit(solution)/shard_map/while
  945.2 45.2 %all-gather.37.cloned.1.call-start = ((), (), s32[]{:S(2)}) async-start(), calls=%async_computation.17 | async-start | bytes 6488064 | tf_op jit(solution)/shard_map/while/body/eval_jaxpr/all_gather | solution.py:243
  946.0 114.6 %all-gather.35.cloned.1.call-start = ((), (), s32[]{:S(2)}) async-start(), calls=%async_computation.16 | async-start | bytes 12976128 | tf_op jit(solution)/shard_map/while/body/eval_jaxpr/all_gather | solution.py:242
  946.6 280.0 %all-reduce.15.cloned.1.call-start = ((), (), s32[]{:S(2)}) async-start(), calls=%async_computation.18 | async-start | bytes 8388608 | tf_op jit(solution)/shard_map/while/body/eval_jaxpr/psum | solution.py:135
  1071.4 183.8 %all-gather.33.cloned.1.call-start = ((), (), s32[]{:S(2)}) async-start(), calls=%async_computation.15 | async-start | bytes 2359296 | tf_op jit(solution)/shard_map/while/body/eval_jaxpr/all_gather | solution.py:241
  1072.0 257.7 %all-gather.39.cloned.1.call-start = ((), (), s32[]{:S(2)}) async-start(), calls=%async_computation.19 | async-start | bytes 2359296 | tf_op jit(solution)/shard_map/while/body/eval_jaxpr/all_gather | solution.py:239
  1298.5 34.2 %collective-permute-start.1 = (f32[512,128]{0,1:T(8,128)S(1)}, f32[512,128]{0,1:T(8,128)S(1)}, u32[]{:S(2)}, u32[]{:S(2)}) collective-permute-start(f32[512,128]{0,1:T(8,128)S(1)} %pad_maximum_fusion.13), channel_id=1, source_target_pairs={{4,0},{5,1},{6,2},{7,3},{12,8},{13,9},{14,10},{15,11},{20,16},{21,... | collective-permute-start | bytes 786440 | tf_op jit(solution)/shard_map/while/body/eval_jaxpr/ppermute | solution.py:16
  1336.6 93.1 %collective-permute-start.2 = (f32[512,2048]{1,0:T(8,128)}, f32[512,2048]{1,0:T(8,128)}, u32[]{:S(2)}, u32[]{:S(2)}) collective-permute-start(f32[512,2048]{1,0:T(8,128)} %convolution_add_fusion.2), channel_id=1, source_target_pairs={{0,1},{1,0},{2,3},{3,2},{4,5},{5,4},{6,7},{7,6},{8,9},{9,8},{10,11... | collective-permute-start | bytes 12582920 | tf_op jit(solution)/shard_map/while/body/eval_jaxpr/ppermute | solution.py:183
  1338.1 100.6 %slice-start.1 = ((s8[5767168]{0:T(1024)(128)(4,1)}), s8[4194304]{0:T(1024)(128)(4,1)S(1)}, s32[]{:S(2)}) async-start(s8[5767168]{0:T(1024)(128)(4,1)} %bitcast.444), calls=%async_computation.21 | async-start | bytes 8388608 | tf_op jit(solution)/shard_map/while
  1338.1 100.6 %copy-start.20 = (bf16[2,512,2048]{2,1,0:T(8,128)(2,1)S(1)}, bf16[2,512,2048]{2,1,0:T(8,128)(2,1)}, u32[]{:S(2)}) copy-start(bf16[2,512,2048]{2,1,0:T(8,128)(2,1)} %get-tuple-element.1384) | copy-start | bytes 12582916 | tf_op jit(solution)/shard_map/while
  1436.2 183.0 %collective-permute-start.3 = (f32[512,2048]{1,0:T(8,128)}, f32[512,2048]{1,0:T(8,128)}, u32[]{:S(2)}, u32[]{:S(2)}) collective-permute-start(f32[512,2048]{1,0:T(8,128)} %add.399), channel_id=1, source_target_pairs={{0,2},{1,3},{2,0},{3,1},{4,6},{5,7},{6,4},{7,5},{8,10},{9,11},{10,... | collective-permute-start | bytes 12582920 | tf_op jit(solution)/shard_map/while/body/eval_jaxpr/ppermute | solution.py:183
  1487.1 137.3 %copy-start.9 = (f32[2048,512]{1,0:T(8,128)}, f32[2048,512]{1,0:T(8,128)S(1)}, u32[]{:S(2)}) copy-start(f32[2048,512]{1,0:T(8,128)S(1)} %select_add_fusion.13) | copy-start | bytes 12582916 | tf_op jit(solution)/shard_map/while
  1487.1 132.1 %copy-start.3 = (bf16[2,512,2048]{2,1,0:T(8,128)(2,1)S(1)}, bf16[2,512,2048]{2,1,0:T(8,128)(2,1)}, u32[]{:S(2)}) copy-start(bf16[2,512,2048]{2,1,0:T(8,128)(2,1)} %get-tuple-element.1397) | copy-start | bytes 12582916 | tf_op jit(solution)/shard_map/while
  1487.1 132.1 %copy-start.33 = (f32[512]{0:T(512)S(1)}, f32[512]{0:T(512)}, u32[]{:S(2)}) copy-start(f32[512]{0:T(512)} %get-tuple-element.1220) | copy-start | bytes 6148 | tf_op jit(solution)/shard_map/while
  1488.4 136.0 %copy-start.15 = (f32[2048,1,128]{2,0,1:T(8,128)}, f32[2048,1,128]{2,0,1:T(8,128)S(1)}, u32[]{:S(2)}) copy-start(f32[2048,1,128]{2,0,1:T(8,128)S(1)} %fusion.273) | copy-start | bytes 3145732 | tf_op jit(solution)/shard_map/while
  1631.1 390.8 %copy-start.10 = (f32[512,64]{0,1:T(8,128)}, f32[512,64]{0,1:T(8,128)S(1)}, u32[]{:S(2)}) copy-start(f32[512,64]{0,1:T(8,128)S(1)} %get-tuple-element.1391) | copy-start | bytes 393220 | tf_op jit(solution)/shard_map/while
  1631.1 47.4 %all-gather.37.cloned.1.call-start = ((), (), s32[]{:S(2)}) async-start(), calls=%async_computation.17 | async-start | bytes 6488064 | tf_op jit(solution)/shard_map/while/body/eval_jaxpr/all_gather | solution.py:243
  1631.7 117.2 %all-gather.35.cloned.1.call-start = ((), (), s32[]{:S(2)}) async-start(), calls=%async_computation.16 | async-start | bytes 12976128 | tf_op jit(solution)/shard_map/while/body/eval_jaxpr/all_gather | solution.py:242
  1632.5 282.3 %all-reduce.15.cloned.1.call-start = ((), (), s32[]{:S(2)}) async-start(), calls=%async_computation.18 | async-start | bytes 8388608 | tf_op jit(solution)/shard_map/while/body/eval_jaxpr/psum | solution.py:135
  1759.7 184.0 %all-gather.33.cloned.1.call-start = ((), (), s32[]{:S(2)}) async-start(), calls=%async_computation.15 | async-start | bytes 2359296 | tf_op jit(solution)/shard_map/while/body/eval_jaxpr/all_gather | solution.py:241
  1760.4 257.5 %all-gather.39.cloned.1.call-start = ((), (), s32[]{:S(2)}) async-start(), calls=%async_computation.19 | async-start | bytes 2359296 | tf_op jit(solution)/shard_map/while/body/eval_jaxpr/all_gather | solution.py:239
  1986.9 34.0 %collective-permute-start.1 = (f32[512,128]{0,1:T(8,128)S(1)}, f32[512,128]{0,1:T(8,128)S(1)}, u32[]{:S(2)}, u32[]{:S(2)}) collective-permute-start(f32[512,128]{0,1:T(8,128)S(1)} %pad_maximum_fusion.13), channel_id=1, source_target_pairs={{4,0},{5,1},{6,2},{7,3},{12,8},{13,9},{14,10},{15,11},{20,16},{21,... | collective-permute-start | bytes 786440 | tf_op jit(solution)/shard_map/while/body/eval_jaxpr/ppermute | solution.py:16
  2024.7 93.0 %collective-permute-start.2 = (f32[512,2048]{1,0:T(8,128)}, f32[512,2048]{1,0:T(8,128)}, u32[]{:S(2)}, u32[]{:S(2)}) collective-permute-start(f32[512,2048]{1,0:T(8,128)} %convolution_add_fusion.2), channel_id=1, source_target_pairs={{0,1},{1,0},{2,3},{3,2},{4,5},{5,4},{6,7},{7,6},{8,9},{9,8},{10,11... | collective-permute-start | bytes 12582920 | tf_op jit(solution)/shard_map/while/body/eval_jaxpr/ppermute | solution.py:183
  2026.2 100.6 %copy-start.20 = (bf16[2,512,2048]{2,1,0:T(8,128)(2,1)S(1)}, bf16[2,512,2048]{2,1,0:T(8,128)(2,1)}, u32[]{:S(2)}) copy-start(bf16[2,512,2048]{2,1,0:T(8,128)(2,1)} %get-tuple-element.1384) | copy-start | bytes 12582916 | tf_op jit(solution)/shard_map/while
  2124.4 183.0 %collective-permute-start.3 = (f32[512,2048]{1,0:T(8,128)}, f32[512,2048]{1,0:T(8,128)}, u32[]{:S(2)}, u32[]{:S(2)}) collective-permute-start(f32[512,2048]{1,0:T(8,128)} %add.399), channel_id=1, source_target_pairs={{0,2},{1,3},{2,0},{3,1},{4,6},{5,7},{6,4},{7,5},{8,10},{9,11},{10,... | collective-permute-start | bytes 12582920 | tf_op jit(solution)/shard_map/while/body/eval_jaxpr/ppermute | solution.py:183
  2182.6 129.9 %copy-start.9 = (f32[2048,512]{1,0:T(8,128)}, f32[2048,512]{1,0:T(8,128)S(1)}, u32[]{:S(2)}) copy-start(f32[2048,512]{1,0:T(8,128)S(1)} %select_add_fusion.13) | copy-start | bytes 12582916 | tf_op jit(solution)/shard_map/while
  2182.6 124.8 %copy-start.3 = (bf16[2,512,2048]{2,1,0:T(8,128)(2,1)S(1)}, bf16[2,512,2048]{2,1,0:T(8,128)(2,1)}, u32[]{:S(2)}) copy-start(bf16[2,512,2048]{2,1,0:T(8,128)(2,1)} %get-tuple-element.1397) | copy-start | bytes 12582916 | tf_op jit(solution)/shard_map/while
  2182.6 124.8 %copy-start.33 = (f32[512]{0:T(512)S(1)}, f32[512]{0:T(512)}, u32[]{:S(2)}) copy-start(f32[512]{0:T(512)} %get-tuple-element.1220) | copy-start | bytes 6148 | tf_op jit(solution)/shard_map/while
  2183.9 128.7 %copy-start.15 = (f32[2048,1,128]{2,0,1:T(8,128)}, f32[2048,1,128]{2,0,1:T(8,128)S(1)}, u32[]{:S(2)}) copy-start(f32[2048,1,128]{2,0,1:T(8,128)S(1)} %fusion.273) | copy-start | bytes 3145732 | tf_op jit(solution)/shard_map/while
  2322.5 327.1 %all-reduce.9.cloned.1.call-start = ((), (), s32[]{:S(2)}) async-start(), calls=%async_computation.8 | async-start | bytes 46137344
  2361.3 328.3 %reduce-scatter.7.cloned.1.call-start = ((), (), s32[]{:S(2)}) async-start(), calls=%async_computation.5 | async-start | bytes 1179648 | tf_op jit(solution)/shard_map/reduce_scatter | solution.py:261
  2361.8 383.1 %reduce-scatter.5.cloned.1.call-start = ((), (), s32[]{:S(2)}) async-start(), calls=%async_computation.4 | async-start | bytes 4718592 | tf_op jit(solution)/shard_map/reduce_scatter | solution.py:260
  2362.4 437.7 %reduce-scatter.9.cloned.1.call-start = ((), (), s32[]{:S(2)}) async-start(), calls=%async_computation.6 | async-start | bytes 4718592 | tf_op jit(solution)/shard_map/reduce_scatter | solution.py:262
  2363.2 528.1 %reduce-scatter.11.cloned.1.call-start = ((), (), s32[]{:S(2)}) async-start(), calls=%async_computation.7 | async-start | bytes 12976128 | tf_op jit(solution)/shard_map/reduce_scatter | solution.py:264
  (87 other events, 1011.5 us)
Sparse Core Ops, SparseCore 0:
  24.0 32.3 all-gather.24
  63.3 27.7 all-gather.26
  101.9 156.1 all-reduce.10
  259.8 66.6 all-gather.30
  328.3 43.3 all-gather.28
  380.9 86.4 all-reduce.12
  483.3 27.5 all-gather.24
  520.7 26.1 all-gather.26
  558.8 155.1 all-reduce.10
  715.8 66.6 all-gather.30
  784.4 43.3 all-gather.28
  837.1 86.4 all-reduce.12
  948.1 42.2 all-gather.36
  992.9 67.6 all-gather.34
  1071.5 154.9 all-reduce.14
  1228.3 26.8 all-gather.32
  1257.0 27.9 all-gather.38
  1633.7 44.7 all-gather.36
  1681.2 67.6 all-gather.34
  1759.8 154.9 all-reduce.14
  1916.7 26.8 all-gather.32
  1945.5 27.9 all-gather.38
Sparse Core Ops, SparseCore 1:
  2361.3 288.2 all-reduce.8
  2653.5 35.9 reduce-scatter.6
  2693.7 51.2 reduce-scatter.4
  2748.9 51.2 reduce-scatter.8
  2804.6 86.6 reduce-scatter.10
